TPU v7x, 128 devices: a whole 4x4x4 slice. The times are simulated.
128 devices in a mesh: row: 16 (over x, z), col: 8 (over y, core).
Axes of the slice: x: 4, y: 4, z: 4, core: 2. Of those that a mesh axis runs over, the one named last changes fastest.
Arguments:
- trailing: bfloat16 [49152, 16384], P('row', 'col'), may hold values from -6 to 6
- panels: bfloat16 [2, 256, 49152], P(None, 'col', 'row'), as said below
- diag_lower: bfloat16 [2, 256, 256], P(None, 'col'), as said below
- pivot_src: int32 [2, 256], replicated, may hold values from 0 to 49151, as said below
- pivot_dst: int32 [2, 256], replicated, may hold values from 256 to 49152, as said below
Outputs:
- matrix: bfloat16 [49152, 16384], P('row', 'col')
Inputs may be any that keep to these rules, and one draw needn't show every extreme that they name: The entries of pivot_src[k] are distinct rows, none below 256 * k. Entries of pivot_dst[k] under 49152 are distinct, not below 256 * (k + 1), and are exactly the entries of pivot_src[k] that are not below 256 * (k + 1); an entry equal to 49152 marks an old row t + j that is itself one of pivot_src[k]. panels[k, c, r] is zero for r < 256 * (k + 1). diag_lower[k, r, c] is zero for c >= r.
All inputs are finite; a program needn't handle non-finite values.
Results may differ from a plain program's by a relative error of at most 0.0062.
Values may be sent and summed in bfloat16 or wider, within the bound.
No kernel may reach another device: no remote copies, remote signals or barrier semaphores. Data moves between devices by JAX's collectives and lax.ppermute only.
A program may use at most 128 MiB of HBM per device.

v0:
```python
import jax
import jax.numpy as jnp
from jax import lax
from jax.sharding import PartitionSpec as P


def broadcast(x, axis, root):
    mine = lax.axis_index(axis) == root
    return lax.psum(jnp.where(mine, x, jnp.zeros_like(x)), axis)


def per_device(trailing, panels, diag_lower, pivot_src, pivot_dst):
    rows_dev, cols_dev = trailing.shape
    panel_width = diag_lower.shape[2]
    row_index = lax.axis_index("row")
    offset = row_index * rows_dev
    identity = jnp.eye(panel_width, dtype=jnp.float32)
    matrix = trailing
    for panel_step in range(pivot_src.shape[0]):
        start_row = panel_step * panel_width
        sources = pivot_src[panel_step] - offset
        holding = (sources >= 0) & (sources < rows_dev)
        picked = jnp.take(matrix, jnp.clip(sources, 0, rows_dev - 1), axis=0)
        picked = jnp.where(holding[:, None], picked, jnp.zeros((), jnp.bfloat16))
        top_rows = matrix[start_row : start_row + panel_width]
        displaced = broadcast(top_rows, "row", 0)
        targets = pivot_dst[panel_step] - offset
        targets = jnp.where((targets >= 0) & (targets < rows_dev), targets, rows_dev)
        swapped = matrix.at[targets].set(displaced, mode="drop")
        factor = lax.all_gather(diag_lower[panel_step], "col", axis=0, tiled=True)
        unit_lower = factor.astype(jnp.float32) + identity
        block_rows = lax.psum(picked, "row").astype(jnp.float32)
        upper_rows = jax.scipy.linalg.solve_triangular(
            unit_lower, block_rows, lower=True, unit_diagonal=True
        ).astype(jnp.bfloat16)
        product = lax.dot_general(
            lax.all_gather(panels[panel_step], "col", axis=0, tiled=True),
            upper_rows,
            (((0,), (0,)), ((), ())),
            preferred_element_type=jnp.float32,
        )
        result = (swapped.astype(jnp.float32) - product).astype(jnp.bfloat16)
        current = result[start_row : start_row + panel_width]
        matrix = result.at[start_row : start_row + panel_width].set(
            jnp.where(row_index == 0, upper_rows, current)
        )
    return matrix


def solution(mesh):
    placed = (P("row", "col"), P(None, "col", "row"), P(None, "col", None), P(), P())
    return jax.shard_map(
        per_device, mesh=mesh, in_specs=placed, out_specs=P("row", "col"), check_vma=False
    )
```

profile of v0, /device:TPU:0, one launch (start us, length us, event | category | flops | bytes accessed | tf_op | source)
XLA Modules:
  0.0 298.3 jit_solution(11988537814029890667)
XLA Ops:
  7.4 0.0 copy-start.3
  7.4 0.0 all-reduce.7.cloned.1.call-start
  7.4 10.7 %copy.35 = bf16[3072,2048]{1,0:T(8,128)(2,1)} copy(bf16[3072,2048]{1,0:T(8,128)(2,1)} %param.13) | data formatting | bytes 25165824
  18.1 0.0 copy-start.1
  18.1 0.0 copy-start.2
  18.1 0.0 copy-start.4
  18.1 0.0 copy-done.3
  18.2 8.6 %gather_fusion = bf16[256,2048]{1,0:T(8,128)(2,1)S(1)} fusion(bf16[3072,2048]{1,0:T(8,128)(2,1)} %copy.35, s32[1024]{0:T(1024)S(1)} %pad_clamp_fusion.1), kind=kCustom, calls=%fused_computation.clone | custom fusion | bytes 2098176 | tf_op jit(solution)/shard_map/jit(_take)/gather | solution.py:23
  26.8 2.8 select_select_fusion.1
  29.7 0.0 all-reduce.7.cloned.1.call-update
  29.7 0.0 all-gather.7.cloned.1.call-start
  29.7 0.0 copy-done.1
  29.7 0.8 fusion.20
  30.5 0.0 all-gather.7.cloned.1.call-update
  30.5 0.0 all-reduce.5.cloned.1.call-start
  30.6 0.0 copy-done.2
  30.6 13.4 %all-gather = bf16[1,256,256]{2,1,0:T(8,128)(2,1)S(1)} all-gather(bf16[1,32,256]{2,1,0:T(8,128)(2,1)S(1)} %get-tuple-element.76), channel_id=2, replica_groups=mesh['row'=16,'col'=8] {'col'}, dimensions={1}, use_global_device_ids=true | all-gather | bytes 147456 | tf_op jit(solution)/shard_map/all_gather | solution.py:30
  44.0 13.0 %all-gather.2 = bf16[1,256,256]{2,1,0:T(8,128)(2,1)S(1)} all-gather(bf16[1,32,256]{2,1,0:T(8,128)(2,1)S(1)} %get-tuple-element.75), channel_id=4, replica_groups=mesh['row'=16,'col'=8] {'col'}, dimensions={1}, use_global_device_ids=true | all-gather | bytes 147456 | tf_op jit(solution)/shard_map/all_gather | solution.py:30
  57.0 0.1 convert_add_fusion
  57.1 0.1 triangular_solve.107
  57.2 4.3 %while.6 = (s32[]{:T(128)}, f32[256,256]{1,0:T(8,128)S(1)}, s32[2,2]{1,0:T(2,128)S(1)}, f32[2,128,128]{2,1,0:T(8,128)S(1)}, s32[]{:T(128)}) while((s32[]{:T(128)}, f32[256,256]{1,0:T(8,128)S(1)}, s32[2,2]{1,0:T(2,128)S(1)}, f32[2,128,128]{2,1,0:T(8,128)S(1)}, s32[]{:T(128)}) %tuple.51), condition=%wide.while_cond.2, body=%wide.while_body.2.sunk | while | flops 2 | bytes 131181 | solution.py:33
  57.3 0.7 fusion.28
  57.9 1.5 bitcast_dynamic-update-slice_fusion.4
  59.4 0.7 fusion.28
  60.1 1.5 bitcast_dynamic-update-slice_fusion.4
  61.6 0.0 copy-start
  61.6 0.0 copy-start.5
  61.6 19.7 %custom-call.4 = f32[2,128,128]{1,2,0:T(8,128)S(1)} custom-call(f32[2,128,128]{2,1,0:T(8,128)S(1)} %get-tuple-element.45), custom_call_target="InvertDiagBlocksLowerTriangular" | custom-call | tf_op jit(solution)/shard_map/jit(_solve_triangular)/triangular_solve | solution.py:33
  81.3 0.0 copy-done.4
  81.3 41.8 %all-reduce.7.cloned.1.call-done = (bf16[256,2048]{1,0:T(8,128)(2,1)}, bf16[256,2048]{1,0:T(8,128)(2,1)}) async-done(((bf16[256,2048]{1,0:T(8,128)(2,1)}, bf16[256,2048]{1,0:T(8,128)(2,1)}), (bf16[256,2048]{1,0:T(8,128)(2,1)}, bf16[256,2048]{1,0:T(8,128)(2,1)})) %all-reduce.7.cloned.1.call-update) | async-done | bytes 2097168 | tf_op jit(solution)/shard_map/psum | solution.py:9
  123.1 0.0 copy-done
  123.1 0.0 copy-done.5
  123.1 1.5 convert_element_type.38
  124.6 15.3 %scatter_fusion = bf16[3072,2048]{1,0:T(8,128)(2,1)} fusion(bf16[3072,2048]{1,0:T(8,128)(2,1)} %copy.35, s32[256]{0:T(256)S(1)} %bitcast.65, bf16[256,2048]{1,0:T(8,128)(2,1)} %get-tuple-element.67), kind=kCustom, calls=%fused_computation.2 | custom fusion | bytes 3146752 | tf_op jit(solution)/shard_map/scatter | solution.py:29
  139.9 1.1 fusion.8
  140.9 1.9 convolution_subtract_fusion.1
  142.8 1.1 fusion.15
  143.9 0.0 all-gather.7.cloned.1.call-done
  143.9 9.9 %fusion.1 = bf16[3072,2048]{1,0:T(8,128)(2,1)} fusion(bf16[3072,2048]{1,0:T(8,128)(2,1)} %scatter_fusion, bf16[1,256,3072]{2,1,0:T(8,128)(2,1)} %all-gather.7.cloned.1.call-done, bf16[128,2048]{1,0:T(8,128)(2,1)S(1)} %fusion.15, f32[128,2048]{1,0:T(8,128)S(1)} %fusion.8), kind=kOutput, calls=%fused_computation.11 | convolution fusion | flops 3242196992 | bytes 28311552 | tf_op jit(solution)/shard_map/dot_general | solution.py:36
  153.8 0.0 copy-start.6
  153.8 2.5 fusion.7
  156.3 2.3 slice_select_fusion.1
  158.6 8.6 %gather_fusion.1 = bf16[256,2048]{1,0:T(8,128)(2,1)S(1)} fusion(bf16[3072,2048]{1,0:T(8,128)(2,1)} %fusion.7, s32[1024]{0:T(1024)S(1)} %pad_clamp_fusion), kind=kCustom, calls=%fused_computation.1.clone | custom fusion | bytes 2098176 | tf_op jit(solution)/shard_map/jit(_take)/gather | solution.py:23
  167.2 1.2 select_select_fusion
  168.4 0.0 all-reduce.5.cloned.1.call-update
  168.4 0.2 all-gather.9.cloned.1.call-start
  168.6 0.4 all-gather.9.cloned.1.call-update
  169.0 0.0 copy-done.6
  169.0 3.8 %while.7 = (s32[]{:T(128)}, f32[256,256]{1,0:T(8,128)S(1)}, s32[2,2]{1,0:T(2,128)S(1)}, f32[2,128,128]{2,1,0:T(8,128)S(1)}, s32[]{:T(128)}) while((s32[]{:T(128)}, f32[256,256]{1,0:T(8,128)S(1)}, s32[2,2]{1,0:T(2,128)S(1)}, f32[2,128,128]{2,1,0:T(8,128)S(1)}, s32[]{:T(128)}) %tuple.67), condition=%wide.while_cond.2.clone, body=%wide.while_body.2.clone.sunk | while | flops 2 | bytes 131181 | solution.py:33
  169.0 0.6 fusion.29
  169.6 1.3 bitcast_dynamic-update-slice_fusion.5
  170.9 0.6 fusion.29
  171.5 1.3 bitcast_dynamic-update-slice_fusion.5
  172.8 19.7 %custom-call.5 = f32[2,128,128]{1,2,0:T(8,128)S(1)} custom-call(f32[2,128,128]{2,1,0:T(8,128)S(1)} %get-tuple-element.46), custom_call_target="InvertDiagBlocksLowerTriangular" | custom-call | tf_op jit(solution)/shard_map/jit(_solve_triangular)/triangular_solve | solution.py:33
  192.5 66.2 %all-reduce.5.cloned.1.call-done = (bf16[256,2048]{1,0:T(8,128)(2,1)}, bf16[256,2048]{1,0:T(8,128)(2,1)}) async-done(((bf16[256,2048]{1,0:T(8,128)(2,1)}, bf16[256,2048]{1,0:T(8,128)(2,1)}), (bf16[256,2048]{1,0:T(8,128)(2,1)}, bf16[256,2048]{1,0:T(8,128)(2,1)})) %all-reduce.5.cloned.1.call-update) | async-done | bytes 2097168 | tf_op jit(solution)/shard_map/psum | solution.py:9
  258.6 1.5 convert_element_type.43
  260.1 15.0 %scatter_fusion.1 = bf16[3072,2048]{1,0:T(8,128)(2,1)} fusion(bf16[3072,2048]{1,0:T(8,128)(2,1)} %fusion.7, s32[256]{0:T(256)S(1)} %bitcast.64, bf16[256,2048]{1,0:T(8,128)(2,1)} %get-tuple-element.65), kind=kCustom, calls=%fused_computation.3 | custom fusion | bytes 3146752 | tf_op jit(solution)/shard_map/scatter | solution.py:29
  275.1 1.1 fusion.5
  276.1 1.0 convolution_subtract_fusion
  277.2 1.1 fusion.13
  278.2 0.0 all-gather.9.cloned.1.call-done
  278.3 9.9 %fusion = bf16[3072,2048]{1,0:T(8,128)(2,1)} fusion(bf16[3072,2048]{1,0:T(8,128)(2,1)} %scatter_fusion.1, bf16[1,256,3072]{2,1,0:T(8,128)(2,1)} %all-gather.9.cloned.1.call-done, bf16[128,2048]{1,0:T(8,128)(2,1)S(1)} %fusion.13, f32[128,2048]{1,0:T(8,128)S(1)} %fusion.5), kind=kOutput, calls=%fused_computation.9 | convolution fusion | flops 3242196992 | bytes 28311552 | tf_op jit(solution)/shard_map/dot_general | solution.py:36
  288.1 2.5 fusion.4
  (18 shorter events, 0.1 us)
Async XLA Ops:
  7.4 10.7 %copy-start.3 = (s32[2,256]{1,0:T(2,128)S(1)}, s32[2,256]{1,0:T(2,128)}, u32[]{:S(2)}) copy-start(s32[2,256]{1,0:T(2,128)} %param.16) | copy-start | bytes 6148
  7.4 115.7 %all-reduce.7.cloned.1.call-start = ((), (), s32[]{:S(2)}) async-start(), calls=%async_computation.3 | async-start | bytes 4194304 | tf_op jit(solution)/shard_map/psum | solution.py:9
  18.1 11.6 %copy-start.1 = (bf16[2,32,3072]{2,1,0:T(8,128)(2,1)S(1)}, bf16[2,32,3072]{2,1,0:T(8,128)(2,1)}, u32[]{:S(2)}) copy-start(bf16[2,32,3072]{2,1,0:T(8,128)(2,1)} %param.14) | copy-start | bytes 1179652
  18.1 12.5 %copy-start.2 = (bf16[2,32,256]{2,1,0:T(8,128)(2,1)S(1)}, bf16[2,32,256]{2,1,0:T(8,128)(2,1)}, u32[]{:S(2)}) copy-start(bf16[2,32,256]{2,1,0:T(8,128)(2,1)} %param.15) | copy-start | bytes 98308
  18.1 63.2 %copy-start.4 = (s32[2,256]{1,0:T(2,128)S(1)}, s32[2,256]{1,0:T(2,128)}, u32[]{:S(2)}) copy-start(s32[2,256]{1,0:T(2,128)} %param.17) | copy-start | bytes 6148
  29.7 114.2 %all-gather.7.cloned.1.call-start = ((), (), s32[]{:S(2)}) async-start(), calls=%async_computation | async-start | bytes 1769472 | tf_op jit(solution)/shard_map/all_gather | solution.py:37
  30.5 228.1 %all-reduce.5.cloned.1.call-start = ((), (), s32[]{:S(2)}) async-start(), calls=%async_computation.2 | async-start | bytes 4194304 | tf_op jit(solution)/shard_map/psum | solution.py:9
  61.6 61.5 %copy-start = (f32[256,256]{1,0:T(8,128)}, f32[256,256]{1,0:T(8,128)S(1)}, u32[]{:S(2)}) copy-start(f32[256,256]{1,0:T(8,128)S(1)} %get-tuple-element.190) | copy-start | bytes 786436
  61.6 61.5 %copy-start.5 = (s32[2,2]{1,0:T(2,128)}, s32[2,2]{1,0:T(2,128)S(1)}, u32[]{:S(2)}) copy-start(s32[2,2]{1,0:T(2,128)S(1)} %get-tuple-element.203) | copy-start | bytes 52
  153.8 15.2 %copy-start.6 = (s32[2,2]{1,0:T(2,128)S(1)}, s32[2,2]{1,0:T(2,128)}, u32[]{:S(2)}) copy-start(s32[2,2]{1,0:T(2,128)} %copy-done.5) | copy-start | bytes 52
  168.4 109.9 %all-gather.9.cloned.1.call-start = ((), (), s32[]{:S(2)}) async-start(), calls=%async_computation.1 | async-start | bytes 1769472 | tf_op jit(solution)/shard_map/all_gather | solution.py:37
Sparse Core Ops, SparseCore 0:
  29.8 93.2 all-reduce.6
  168.5 90.0 all-reduce.4
Sparse Core Ops, SparseCore 1:
  31.9 26.9 all-gather.6
  170.6 23.8 all-gather.8
where the time goes:
time: 303 us; the launch traced here: 298 us
  waiting for transfers between devices  108 us (36%)
  local copies, waits for them, and re-layouts  67.1 us (22%)
  other arithmetic  53.9 us (18%)
  matrix products  26.8 us (9%)
  blocking collectives  26.4 us (9%)
  between operations  15.4 us (5%)
    psum x2, waiting for transfers between devices, broadcast(): return lax.psum(jnp.where(mine, x, jnp.zeros_like(x)), axis)  108 us
    another operation x5, other arithmetic, per_device(): jax.scipy.linalg.solve_triangular(unit_lower, block_rows, lower=True, uni...  39.5 us
    scatter x2, local copies, waits for them, and re-layouts, per_device(): swapped = matrix.at[targets].set(displaced, mode='drop')  30.3 us
    all_gather x2, blocking collectives, per_device(): factor = lax.all_gather(diag_lower[panel_step], 'col', axis=0, tiled=True)  26.4 us
    dot_general x2, matrix products, per_device(): lax.dot_general(lax.all_gather(panels[panel_step], 'col', axis=0, tiled=T...  19.8 us
    gather x2, local copies, waits for them, and re-layouts, per_device(): picked = jnp.take(matrix, jnp.clip(sources, 0, rows_dev - 1), axis=0)  17.2 us
    unnamed x15, local copies, waits for them, and re-layouts  10.8 us
    another operation x15, local copies, waits for them, and re-layouts, per_device(): jax.scipy.linalg.solve_triangular(unit_lower, block_rows, lower=True, uni...  8.1 us
  transfers between devices with their start and end apart: 4, of which 2 were waited for; matrix products, arithmetic and copies ran while one was open for 30% of the time, Pallas kernels for 0%

commit v1 on v0

--- a/solution.py
+++ b/solution.py
@@ -6,7 +6,7 @@
 
 def broadcast(x, axis, root):
     mine = lax.axis_index(axis) == root
-    return lax.psum(jnp.where(mine, x, jnp.zeros_like(x)), axis)
+    return jnp.sum(lax.all_gather(jnp.where(mine, x, jnp.zeros_like(x)), axis), axis=0)
 
 
 def per_device(trailing, panels, diag_lower, pivot_src, pivot_dst):

time: 303 us -> 529 us (1.75)
  waiting for transfers between devices: 108 us -> 317 us
  other arithmetic: 53.9 us -> 73.1 us
    all_gather x0 -> x2, waiting for transfers between devices: none -> 216 us  [broadcast(): lax.all_gather(jnp.where(mine, x, jnp.zeros_like(x)), axis)]
    reduce_sum x0 -> x2, other arithmetic: none -> 18.5 us  [broadcast(): jnp.sum(lax.all_gather(jnp.where(mine, x, jnp.zeros_like(x)), axis), axis=0)]
    psum x2, waiting for transfers between devices: 108 us -> 97.2 us  [per_device(): block_rows = lax.psum(picked, 'row').astype(jnp.float32)]
    unnamed x15 -> x9, local copies, waits for them, and re-layouts: 10.8 us -> 10.7 us
  transfers between devices with their start and end apart: 4 -> 6, of which waited for: 2 -> 6; matrix products, arithmetic and copies ran while one was open for 30% -> 21% of each run, Pallas kernels for 0% -> 0%
where the time goes in v1:
time: 529 us; the launch traced here: 523 us
  waiting for transfers between devices  317 us (60%)
  other arithmetic  73.1 us (14%)
  local copies, waits for them, and re-layouts  65.7 us (12%)
  blocking collectives  26.6 us (5%)
  matrix products  26 us (5%)
  between operations  14 us (3%)
    all_gather x2, waiting for transfers between devices, broadcast(): lax.all_gather(jnp.where(mine, x, jnp.zeros_like(x)), axis)  216 us
    psum x2, waiting for transfers between devices, per_device(): block_rows = lax.psum(picked, 'row').astype(jnp.float32)  97.2 us
    another operation x5, other arithmetic, per_device(): jax.scipy.linalg.solve_triangular(unit_lower, block_rows, lower=True, uni...  39.5 us
    scatter x2, local copies, waits for them, and re-layouts, per_device(): swapped = matrix.at[targets].set(displaced, mode='drop')  29.1 us
    all_gather x2, blocking collectives, per_device(): factor = lax.all_gather(diag_lower[panel_step], 'col', axis=0, tiled=True)  26.6 us
    dot_general x2, matrix products, per_device(): lax.dot_general(lax.all_gather(panels[panel_step], 'col', axis=0, tiled=T...  19.7 us
    reduce_sum x2, other arithmetic, broadcast(): jnp.sum(lax.all_gather(jnp.where(mine, x, jnp.zeros_like(x)), axis), axis=0)  18.5 us
    gather x2, local copies, waits for them, and re-layouts, per_device(): picked = jnp.take(matrix, jnp.clip(sources, 0, rows_dev - 1), axis=0)  17.2 us
  transfers between devices with their start and end apart: 6, of which 6 were waited for; matrix products, arithmetic and copies ran while one was open for 21% of the time, Pallas kernels for 0%

profile of v1, /device:TPU:0, one launch (start us, length us, event | category | flops | bytes accessed | tf_op | source)
XLA Modules:
  0.0 523.2 jit_solution(830308207915799835)
XLA Ops:
  6.5 0.0 copy-start.2
  6.5 0.0 all-reduce.3.cloned.1.call-start
  6.5 10.7 %copy.33 = bf16[3072,2048]{1,0:T(8,128)(2,1)} copy(bf16[3072,2048]{1,0:T(8,128)(2,1)} %param.13) | data formatting | bytes 25165824
  17.3 0.0 copy-start
  17.3 0.0 copy-done.2
  17.4 8.6 %gather_fusion = bf16[256,2048]{1,0:T(8,128)(2,1)S(1)} fusion(bf16[3072,2048]{1,0:T(8,128)(2,1)} %copy.33, s32[1024]{0:T(1024)S(1)} %pad_clamp_fusion.1), kind=kCustom, calls=%fused_computation.clone | custom fusion | bytes 2098176 | tf_op jit(solution)/shard_map/jit(_take)/gather | solution.py:23
  26.0 1.2 select_select_fusion.1
  27.2 0.0 all-reduce.3.cloned.1.call-update
  27.2 0.0 all-gather.11.cloned.1.call-start
  27.3 2.3 slice_select_fusion.3
  29.6 0.0 all-gather.11.cloned.1.call-update
  29.6 0.0 all-gather.13.cloned.1.call-start
  29.6 0.0 copy-done
  29.6 0.8 fusion.20
  30.4 0.0 all-gather.13.cloned.1.call-update
  30.5 0.0 all-reduce.5.cloned.1.call-start
  30.5 0.0 copy-done.1
  30.6 13.4 %all-gather.4 = bf16[1,256,256]{2,1,0:T(8,128)(2,1)S(1)} all-gather(bf16[1,32,256]{2,1,0:T(8,128)(2,1)S(1)} %get-tuple-element.71), channel_id=6, replica_groups=mesh['row'=16,'col'=8] {'col'}, dimensions={1}, use_global_device_ids=true | all-gather | bytes 147456 | tf_op jit(solution)/shard_map/all_gather | solution.py:30
  43.9 13.3 %all-gather.1 = bf16[1,256,256]{2,1,0:T(8,128)(2,1)S(1)} all-gather(bf16[1,32,256]{2,1,0:T(8,128)(2,1)S(1)} %get-tuple-element.72), channel_id=3, replica_groups=mesh['row'=16,'col'=8] {'col'}, dimensions={1}, use_global_device_ids=true | all-gather | bytes 147456 | tf_op jit(solution)/shard_map/all_gather | solution.py:30
  57.2 0.1 convert_add_fusion
  57.3 0.1 triangular_solve.107
  57.4 3.9 while.6
  57.4 0.6 fusion.28
  58.0 1.3 bitcast_dynamic-update-slice_fusion.4
  59.3 0.6 fusion.28
  59.9 1.3 bitcast_dynamic-update-slice_fusion.4
  61.3 19.7 %custom-call.4 = f32[2,128,128]{1,2,0:T(8,128)S(1)} custom-call(f32[2,128,128]{2,1,0:T(8,128)S(1)} %get-tuple-element.45), custom_call_target="InvertDiagBlocksLowerTriangular" | custom-call | tf_op jit(solution)/shard_map/jit(_solve_triangular)/triangular_solve | solution.py:33
  81.0 0.0 copy-done.3
  81.0 36.2 %all-reduce.3.cloned.1.call-done = bf16[256,2048]{1,0:T(8,128)(2,1)} async-done(((bf16[256,2048]{1,0:T(8,128)(2,1)}), bf16[256,2048]{1,0:T(8,128)(2,1)}) %all-reduce.3.cloned.1.call-update) | async-done | bytes 1048592 | tf_op jit(solution)/shard_map/psum | solution.py:32
  117.2 1.5 convert_element_type.42
  118.7 1.1 fusion.8
  119.7 1.0 convolution_subtract_fusion.1
  120.8 1.1 fusion.15
  121.8 108.2 %all-gather.11.cloned.1.call-done = bf16[4096,2048]{1,0:T(8,128)(2,1)} async-done(((bf16[256,2048]{1,0:T(8,128)(2,1)}), bf16[4096,2048]{1,0:T(8,128)(2,1)}) %all-gather.11.cloned.1.call-update) | async-done | bytes 16777232 | tf_op jit(solution)/shard_map/all_gather | solution.py:9
  230.0 9.3 %reduce_sum.24 = bf16[256,2048]{1,0:T(8,128)(2,1)S(1)} reduce(bf16[16,256,2048]{2,1,0:T(8,128)(2,1)} %bitcast.66, bf16[]{:T(256)} %constant.91.clone.1), dimensions={0}, to_apply=%region_0.1 | reduce | flops 7864320 | bytes 17825794 | tf_op jit(solution)/shard_map/reduce_sum | solution.py:9
  239.3 14.5 %scatter_fusion = bf16[3072,2048]{1,0:T(8,128)(2,1)} fusion(bf16[3072,2048]{1,0:T(8,128)(2,1)} %copy.33, s32[256]{0:T(256)S(1)} %bitcast.69, bf16[256,2048]{1,0:T(8,128)(2,1)S(1)} %reduce_sum.24), kind=kCustom, calls=%fused_computation.2 | custom fusion | bytes 3146752 | tf_op jit(solution)/shard_map/scatter | solution.py:29
  253.8 1.8 all-gather.13.cloned.1.call-done
  255.7 9.9 %fusion.1 = bf16[3072,2048]{1,0:T(8,128)(2,1)} fusion(bf16[3072,2048]{1,0:T(8,128)(2,1)} %scatter_fusion, bf16[1,256,3072]{2,1,0:T(8,128)(2,1)} %all-gather.13.cloned.1.call-done, bf16[128,2048]{1,0:T(8,128)(2,1)S(1)} %fusion.15, f32[128,2048]{1,0:T(8,128)S(1)} %fusion.8), kind=kOutput, calls=%fused_computation.11 | convolution fusion | flops 3242196992 | bytes 28311552 | tf_op jit(solution)/shard_map/dot_general | solution.py:36
  265.5 2.5 fusion.7
  268.1 8.6 %gather_fusion.1 = bf16[256,2048]{1,0:T(8,128)(2,1)S(1)} fusion(bf16[3072,2048]{1,0:T(8,128)(2,1)} %fusion.7, s32[1024]{0:T(1024)S(1)} %pad_clamp_fusion), kind=kCustom, calls=%fused_computation.1.clone | custom fusion | bytes 2098176 | tf_op jit(solution)/shard_map/jit(_take)/gather | solution.py:23
  276.6 1.2 select_select_fusion
  277.8 0.0 all-reduce.5.cloned.1.call-update
  277.8 0.0 all-gather.15.cloned.1.call-start
  277.9 2.3 slice_select_fusion.1
  280.2 0.0 all-gather.15.cloned.1.call-update
  280.2 0.3 all-gather.17.cloned.1.call-start
  280.5 0.3 all-gather.17.cloned.1.call-update
  280.8 4.1 while.7
  280.8 0.6 fusion.29
  281.5 1.3 bitcast_dynamic-update-slice_fusion.5
  282.9 0.6 fusion.29
  283.5 1.3 bitcast_dynamic-update-slice_fusion.5
  284.9 19.7 %custom-call.5 = f32[2,128,128]{1,2,0:T(8,128)S(1)} custom-call(f32[2,128,128]{2,1,0:T(8,128)S(1)} %get-tuple-element.46), custom_call_target="InvertDiagBlocksLowerTriangular" | custom-call | tf_op jit(solution)/shard_map/jit(_solve_triangular)/triangular_solve | solution.py:33
  304.6 61.0 %all-reduce.5.cloned.1.call-done = bf16[256,2048]{1,0:T(8,128)(2,1)} async-done(((bf16[256,2048]{1,0:T(8,128)(2,1)}), bf16[256,2048]{1,0:T(8,128)(2,1)}) %all-reduce.5.cloned.1.call-update) | async-done | bytes 1048592 | tf_op jit(solution)/shard_map/psum | solution.py:32
  365.5 1.5 convert_element_type.47
  367.0 1.1 fusion.5
  368.1 1.0 convolution_subtract_fusion
  369.1 1.1 fusion.13
  370.1 108.0 %all-gather.15.cloned.1.call-done = bf16[4096,2048]{1,0:T(8,128)(2,1)} async-done(((bf16[256,2048]{1,0:T(8,128)(2,1)}), bf16[4096,2048]{1,0:T(8,128)(2,1)}) %all-gather.15.cloned.1.call-update) | async-done | bytes 16777232 | tf_op jit(solution)/shard_map/all_gather | solution.py:9
  478.2 9.3 %reduce_sum.25 = bf16[256,2048]{1,0:T(8,128)(2,1)S(1)} reduce(bf16[16,256,2048]{2,1,0:T(8,128)(2,1)} %bitcast.67, bf16[]{:T(256)} %constant.91.clone.1), dimensions={0}, to_apply=%region_3.6 | reduce | flops 7864320 | bytes 17825794 | tf_op jit(solution)/shard_map/reduce_sum | solution.py:9
  487.5 14.6 %scatter_fusion.1 = bf16[3072,2048]{1,0:T(8,128)(2,1)} fusion(bf16[3072,2048]{1,0:T(8,128)(2,1)} %fusion.7, s32[256]{0:T(256)S(1)} %bitcast.68, bf16[256,2048]{1,0:T(8,128)(2,1)S(1)} %reduce_sum.25), kind=kCustom, calls=%fused_computation.3 | custom fusion | bytes 3146752 | tf_op jit(solution)/shard_map/scatter | solution.py:29
  502.0 1.6 all-gather.17.cloned.1.call-done
  503.7 9.9 %fusion = bf16[3072,2048]{1,0:T(8,128)(2,1)} fusion(bf16[3072,2048]{1,0:T(8,128)(2,1)} %scatter_fusion.1, bf16[1,256,3072]{2,1,0:T(8,128)(2,1)} %all-gather.17.cloned.1.call-done, bf16[128,2048]{1,0:T(8,128)(2,1)S(1)} %fusion.13, f32[128,2048]{1,0:T(8,128)S(1)} %fusion.5), kind=kOutput, calls=%fused_computation.9 | convolution fusion | flops 3242196992 | bytes 28311552 | tf_op jit(solution)/shard_map/dot_general | solution.py:36
  513.5 2.5 fusion.4
  (20 shorter events, 0.1 us)
Async XLA Ops:
  6.5 10.7 %copy-start.2 = (s32[2,256]{1,0:T(2,128)S(1)}, s32[2,256]{1,0:T(2,128)}, u32[]{:S(2)}) copy-start(s32[2,256]{1,0:T(2,128)} %param.16) | copy-start | bytes 6148
  6.5 110.7 %all-reduce.3.cloned.1.call-start = ((), (), s32[]{:S(2)}) async-start(), calls=%async_computation | async-start | bytes 2097152 | tf_op jit(solution)/shard_map/psum | solution.py:32
  17.3 12.4 %copy-start = (bf16[2,32,3072]{2,1,0:T(8,128)(2,1)S(1)}, bf16[2,32,3072]{2,1,0:T(8,128)(2,1)}, u32[]{:S(2)}) copy-start(bf16[2,32,3072]{2,1,0:T(8,128)(2,1)} %param.14) | copy-start | bytes 1179652
  17.3 13.3 %copy-start.1 = (bf16[2,32,256]{2,1,0:T(8,128)(2,1)S(1)}, bf16[2,32,256]{2,1,0:T(8,128)(2,1)}, u32[]{:S(2)}) copy-start(bf16[2,32,256]{2,1,0:T(8,128)(2,1)} %param.15) | copy-start | bytes 98308
  17.3 63.7 %copy-start.3 = (s32[2,256]{1,0:T(2,128)S(1)}, s32[2,256]{1,0:T(2,128)}, u32[]{:S(2)}) copy-start(s32[2,256]{1,0:T(2,128)} %param.17) | copy-start | bytes 6148
  27.2 202.8 %all-gather.11.cloned.1.call-start = ((), (), s32[]{:S(2)}) async-start(), calls=%async_computation.2 | async-start | bytes 17825792 | tf_op jit(solution)/shard_map/all_gather | solution.py:9
  29.6 226.1 %all-gather.13.cloned.1.call-start = ((), (), s32[]{:S(2)}) async-start(), calls=%async_computation.3 | async-start | bytes 1769472 | tf_op jit(solution)/shard_map/all_gather | solution.py:37
  30.5 335.1 %all-reduce.5.cloned.1.call-start = ((), (), s32[]{:S(2)}) async-start(), calls=%async_computation.1 | async-start | bytes 2097152 | tf_op jit(solution)/shard_map/psum | solution.py:32
  277.8 200.3 %all-gather.15.cloned.1.call-start = ((), (), s32[]{:S(2)}) async-start(), calls=%async_computation.4 | async-start | bytes 17825792 | tf_op jit(solution)/shard_map/all_gather | solution.py:9
  280.2 223.4 %all-gather.17.cloned.1.call-start = ((), (), s32[]{:S(2)}) async-start(), calls=%async_computation.5 | async-start | bytes 1769472 | tf_op jit(solution)/shard_map/all_gather | solution.py:37
Sparse Core Ops, SparseCore 0:
  27.3 89.8 all-reduce.2
  119.4 110.6 all-gather.10
  231.7 23.8 all-gather.12
  278.0 87.5 all-reduce.4
  367.5 110.6 all-gather.14
  479.7 23.8 all-gather.16
